TPU v7x, 32 devices: a whole 2x2x4 slice. The times are simulated.
32 devices in a mesh: gx: 2 (over core), gy: 4 (over y, x), gz: 4 (over z).
Axes of the slice: x: 2, y: 2, z: 4, core: 2. Of those that a mesh axis runs over, the one named last changes fastest.
Arguments:
- right_side: float32 [96, 192, 192], P('gx', 'gy', 'gz'), may hold values from -6 to 6
- start_guess: float32 [96, 192, 192], P('gx', 'gy', 'gz'), may hold values from -3 to 3
- reaction: float32 [96, 192, 192], P('gx', 'gy', 'gz'), may hold values from 0.0005 to 0.005
Outputs:
- solution_field: float32 [96, 192, 192], P('gx', 'gy', 'gz')
- residual: float32 [96, 192, 192], P('gx', 'gy', 'gz')
All inputs are finite; a program needn't handle non-finite values.
Results may differ from a plain program's by a relative error of at most 0.0003.
Values sent between devices are 32-bit elements.
A program may use at most 128 MiB of HBM per device.

v0:
```python
import jax
import jax.numpy as jnp
from jax import lax
from jax.sharding import PartitionSpec as P

LEVELS = 5
BOTTOM_ITERS = 6


damping = 6.0 / 7.0


def extended(block, sides, width, periodic):
    for axis, dim in sides:
        count = lax.axis_size(axis)
        forward = [(i, i + 1) for i in range(count - 1)]
        if periodic:
            forward.append((count - 1, 0))
        backward = [(target, source) for source, target in forward]
        low = lax.ppermute(
            lax.slice_in_dim(block, block.shape[dim] - width, None, axis=dim), axis, forward
        )
        high = lax.ppermute(lax.slice_in_dim(block, 0, width, axis=dim), axis, backward)
        block = jnp.concatenate([low, block, high], axis=dim)
    return block


def stencil(padded, values, shifted, factor):
    beside = padded[2:, 1:-1, 1:-1] + padded[:-2, 1:-1, 1:-1]
    beside = beside + padded[1:-1, 2:, 1:-1] + padded[1:-1, :-2, 1:-1]
    beside = beside + padded[1:-1, 1:-1, 2:] + padded[1:-1, 1:-1, :-2]
    return factor * (6.0 * values - beside) + shifted * values


def operate_fine(values, shifted, factor):
    padded = extended(values, (("gx", 0), ("gy", 1), ("gz", 2)), 1, False)
    return stencil(padded, values, shifted, factor)


def operate_coarse(values, shifted, factor):
    padded = extended(values, (("gx", 0), ("gy", 1), ("gz", 2)), 1, False)
    return stencil(padded, values, shifted, factor)


def operate_whole(values, shifted, factor):
    return stencil(jnp.pad(values, 1), values, shifted, factor)


def coarsen(values):
    size_x, size_y, size_z = values.shape
    blocks = values.reshape(size_x // 2, 2, size_y // 2, 2, size_z // 2, 2)
    return jnp.mean(blocks, axis=(1, 3, 5))


def refine(values):
    size_x, size_y, size_z = values.shape
    spread = jnp.broadcast_to(values[:, None, :, None, :, None], (size_x, 2, size_y, 2, size_z, 2))
    return spread.reshape(2 * size_x, 2 * size_y, 2 * size_z)


def solve_whole(source, shifted, factor):
    estimate = jnp.zeros_like(source)
    leftover = source
    direction = source
    norm_now = jnp.sum(leftover * leftover)
    for repeat_index in range(BOTTOM_ITERS):
        applied = operate_whole(direction, shifted, factor)
        step_length = norm_now / jnp.sum(direction * applied)
        estimate = estimate + step_length * direction
        leftover = leftover - step_length * applied
        norm_next = jnp.sum(leftover * leftover)
        direction = leftover + norm_next / norm_now * direction
        norm_now = norm_next
    return estimate


def bottom(source, shifted, factor):
    gathered = (
        lax.all_gather(source, "gx", axis=0, tiled=True),
        lax.all_gather(shifted, "gx", axis=0, tiled=True),
    )
    gathered = (
        lax.all_gather(gathered[0], "gy", axis=1, tiled=True),
        lax.all_gather(gathered[1], "gy", axis=1, tiled=True),
    )
    gathered = (
        lax.all_gather(gathered[0], "gz", axis=2, tiled=True),
        lax.all_gather(gathered[1], "gz", axis=2, tiled=True),
    )
    answer = solve_whole(gathered[0], gathered[1], factor)
    size_x, size_y, size_z = source.shape
    corner = (
        lax.axis_index("gx") * size_x,
        lax.axis_index("gy") * size_y,
        lax.axis_index("gz") * size_z,
    )
    return lax.dynamic_slice(answer, corner, (size_x, size_y, size_z))


def vcycle_level(source, shifts, depth_index):
    factor = 0.25**depth_index
    shifted = shifts[depth_index]
    if depth_index == LEVELS - 1:
        return bottom(source, shifted, factor)
    operator = operate_fine if depth_index == 0 else operate_coarse
    diagonal = 6.0 * factor + shifted
    estimate = damping * source / diagonal
    estimate = estimate + damping * (source - operator(estimate, shifted, factor)) / diagonal
    leftover = source - operator(estimate, shifted, factor)
    estimate = estimate + refine(vcycle_level(coarsen(leftover), shifts, depth_index + 1))
    for repeat_index in range(2):
        estimate = estimate + damping * (source - operator(estimate, shifted, factor)) / diagonal
    return estimate


def body(right_side, start_guess, reaction):
    shifts = [reaction]
    for depth_index in range(LEVELS - 1):
        shifts.append(coarsen(shifts[-1]))
    start_residual = right_side - operate_fine(start_guess, reaction, 1.0)
    precond = vcycle_level(start_residual, shifts, 0)
    upper = lax.psum(jnp.sum(start_residual * precond), ("gx", "gy", "gz"))
    applied = operate_fine(precond, reaction, 1.0)
    step_length = upper / lax.psum(jnp.sum(precond * applied), ("gx", "gy", "gz"))
    solution_field = start_guess + step_length * precond
    residual = start_residual - step_length * applied
    return (solution_field, residual)


def solution(mesh):
    placed = (P("gx", "gy", "gz"), P("gx", "gy", "gz"), P("gx", "gy", "gz"))
    return jax.shard_map(
        body,
        mesh=mesh,
        in_specs=placed,
        out_specs=(P("gx", "gy", "gz"), P("gx", "gy", "gz")),
        check_vma=False,
    )
```

profile of v0, /device:TPU:0, one launch (start us, length us, event | category | flops | bytes accessed | tf_op | source)
XLA Modules:
  0.0 805.3 jit_solution(15751533114436817655)
XLA Ops:
  8.8 4.9 collective-permute-start.3
  29.4 8.1 %multiply_divide_fusion = (f32[48,48,48]{2,1,0:T(8,128)S(1)}, f32[48,48,48]{2,1,0:T(8,128)S(1)}) fusion(f32[48,48,48]{2,1,0:T(8,128)S(1)} %copy-done, f32[48,48,48]{2,1,0:T(8,128)} %param.3, f32[48,48,48]{2,1,0:T(8,128)} %param.4, f32[50,1,48]{2,1,0:T(1,128)} %copy-done.35, f32[50,48,48]{2,1,0:T(8,128)} %copy-done.10, f32[50,1,48]{2,1,0:T(1,128)} %copy-done.41, ...), kind=kLoop, calls=%fused_computation.166 | loop fusion | flops 2543616 | bytes 2730272 | tf_op jit(solution)/shard_map/div | solution.py:107
  44.1 5.4 collective-permute-start.9
  67.0 9.3 %fusion.43 = f32[48,48,48]{2,1,0:T(8,128)S(1)} fusion(f32[48,48,48]{2,1,0:T(8,128)} %copy-done.3, f32[48,48,48]{2,1,0:T(8,128)S(1)} %get-tuple-element.23, f32[50,50,1]{2,1,0:T(8,128)} %copy.12, f32[50,1,48]{2,1,0:T(1,128)} %copy-done.38, f32[50,1,48]{2,1,0:T(1,128)} %copy-done.44, f32[1,48,48]{2,1,0:T(8,128)} %copy-done.27, f32[1,48,48]{2,1,0:T(8,128)} %copy-done.31, ...), kind=kLoop, calls=%fused_computation.122 | loop fusion | flops 3538944 | bytes 1827104 | tf_op jit(solution)/shard_map/add | solution.py:108
  82.8 5.7 collective-permute-start.15
  99.2 5.7 collective-permute-start.17
  104.9 13.7 %reshape.48 = f32[24,2,24,2,24,2]{5,4,3,2,1,0:T(8,128)} reshape(f32[48,48,48]{2,1,0:T(8,128)S(1)} %copy-done) | data formatting | bytes 884736 | tf_op jit(solution)/shard_map/reshape | solution.py:51
  118.6 10.9 %reduce_sum.199 = f32[24,24,24]{2,1,0:T(8,128)} reduce(f32[24,2,24,2,24,2]{5,4,3,2,1,0:T(8,128)} %reshape.48, f32[]{:T(128)} %constant.22.clone.1), dimensions={1,3,5}, to_apply=%region_1.0 | reduce | flops 96768 | bytes 497668 | tf_op jit(solution)/shard_map/reduce_sum | solution.py:52
  134.3 6.9 fusion.32
  141.2 15.3 %reshape.47 = f32[24,2,24,2,24,2]{5,4,3,2,1,0:T(8,128)} reshape(f32[48,48,48]{2,1,0:T(8,128)} %fusion.32) | data formatting | bytes 884736 | tf_op jit(solution)/shard_map/reshape | solution.py:51
  156.5 10.9 %reduce_sum.198 = f32[24,24,24]{2,1,0:T(8,128)} reduce(f32[24,2,24,2,24,2]{5,4,3,2,1,0:T(8,128)} %reshape.47, f32[]{:T(128)} %constant.22.clone.1), dimensions={1,3,5}, to_apply=%region_0.0 | reduce | flops 96768 | bytes 497668 | tf_op jit(solution)/shard_map/reduce_sum | solution.py:52
  175.7 5.9 collective-permute-start.21
  189.1 7.2 collective-permute-done.22
  204.5 5.7 collective-permute-start.27
  214.6 5.8 collective-permute-start.29
  247.9 5.4 collective-permute-start.33
  256.1 5.1 collective-permute-start.35
  273.2 6.0 collective-permute-start.39
  283.1 5.8 collective-permute-start.41
  308.4 6.3 collective-permute-start.45
  336.4 5.8 collective-permute-start.51
  342.2 10.4 %all_gather.22 = f32[6,12,3]{0,2,1:T(4,128)} all-gather(f32[6,3,3]{0,2,1:T(4,128)} %copy.19), channel_id=1, replica_groups=mesh['gx'=2,'gy'=4,'gz'=4] {'gy'}, dimensions={1}, use_global_device_ids=true | all-gather | bytes 1080 | tf_op jit(solution)/shard_map/all_gather | solution.py:84
  355.6 4.9 collective-permute-start.53
  360.5 14.9 %all_gather.23 = f32[6,12,12]{1,0,2:T(8,128)} all-gather(f32[6,12,3]{1,0,2:T(8,128)S(1)} %copy.20), channel_id=1, replica_groups=mesh['gx'=2,'gy'=4,'gz'=4] {'gz'}, dimensions={2}, use_global_device_ids=true | all-gather | bytes 4320 | tf_op jit(solution)/shard_map/all_gather | solution.py:88
  382.1 8.5 %all_gather.19 = f32[6,12,3]{0,2,1:T(4,128)} all-gather(f32[6,3,3]{0,2,1:T(4,128)} %copy.17), channel_id=1, replica_groups=mesh['gx'=2,'gy'=4,'gz'=4] {'gy'}, dimensions={1}, use_global_device_ids=true | all-gather | bytes 1080 | tf_op jit(solution)/shard_map/all_gather | solution.py:83
  391.5 13.1 %all_gather.20 = f32[6,12,12]{1,0,2:T(8,128)S(1)} all-gather(f32[6,12,3]{1,0,2:T(8,128)S(1)} %copy.18), channel_id=1, replica_groups=mesh['gx'=2,'gy'=4,'gz'=4] {'gz'}, dimensions={2}, use_global_device_ids=true | all-gather | bytes 4320 | tf_op jit(solution)/shard_map/all_gather | solution.py:87
  486.0 4.9 collective-permute-start.65
  503.6 5.6 collective-permute-start.69
  512.0 4.9 collective-permute-start.71
  525.9 5.7 collective-permute-start.75
  534.4 5.0 collective-permute-start.77
  556.4 5.8 collective-permute-start.81
  565.2 5.0 collective-permute-start.83
  570.2 7.5 collective-permute-done.82
  585.9 5.7 collective-permute-start.87
  594.6 5.3 collective-permute-start.89
  599.9 7.3 collective-permute-done.88
  608.8 9.7 %broadcast_in_dim.11 = f32[24,2,24,2,24,2]{5,4,3,2,1,0:T(8,128)} broadcast(f32[24,24,24]{2,1,0:T(8,128)S(1)} %fusion.63), dimensions={0,2,4} | broadcast | bytes 497664 | tf_op jit(solution)/shard_map/broadcast_in_dim | solution.py:57
  618.5 17.3 %reshape.55 = f32[48,48,48]{2,1,0:T(8,128)} reshape(f32[24,2,24,2,24,2]{5,4,3,2,1,0:T(8,128)} %broadcast_in_dim.11) | data formatting | bytes 884736 | tf_op jit(solution)/shard_map/reshape | solution.py:58
  643.7 5.4 collective-permute-start.93
  659.5 5.8 collective-permute-start.95
  670.1 6.2 fusion.24
  682.9 5.4 collective-permute-start.99
  705.6 9.3 %fusion.13 = f32[48,48,48]{2,1,0:T(8,128)S(1)} fusion(f32[48,48,48]{2,1,0:T(8,128)} %copy-done.4, f32[48,48,48]{2,1,0:T(8,128)S(1)} %get-tuple-element.23, f32[50,50,1]{2,1,0:T(8,128)} %copy.29, f32[50,1,48]{2,1,0:T(1,128)} %copy-done.40, f32[50,1,48]{2,1,0:T(1,128)} %copy-done.46, f32[1,48,48]{2,1,0:T(8,128)} %copy-done.29, f32[1,48,48]{2,1,0:T(8,128)} %copy-done.33, ...), kind=kLoop, calls=%fused_computation.38 | loop fusion | flops 3538944 | bytes 1827104 | tf_op jit(solution)/shard_map/add | solution.py:112
  721.5 6.0 collective-permute-start.105
  737.8 5.2 collective-permute-start.107
  747.9 7.7 multiply_reduce_fusion
  755.7 44.6 %all-reduce.6 = (f32[]{:T(128)}, f32[]{:T(128)}) all-reduce(f32[]{:T(128)} %get-tuple-element.3, f32[]{:T(128)} %get-tuple-element.2), channel_id=1, replica_groups=mesh['gx'=2,'gy'=4,'gz'=4] {'gx','gy','gz'}, use_global_device_ids=true, to_apply=%region_21.22 | all-reduce | flops 2 | bytes 16 | tf_op jit(solution)/shard_map/psum | solution.py:122
  (452 shorter events, 394.4 us)
Async XLA Ops:
  55.7 7.9 collective-permute-start.10
  81.5 7.1 collective-permute-start.14
  82.8 7.3 collective-permute-start.15
  95.4 34.0 %collective-permute-start.16 = (f32[50,50,1]{1,2,0:T(1,128)}, f32[50,50,1]{1,2,0:T(1,128)}, u32[]{:S(2)}, u32[]{:S(2)}) collective-permute-start(f32[50,50,1]{1,2,0:T(1,128)} %copy.13), channel_id=1, source_target_pairs={{1,0},{2,1},{3,2},{5,4},{6,5},{7,6},{9,8},{10,9},{11,10},{13,12},{... | collective-permute-start | bytes 30008 | tf_op jit(solution)/shard_map/ppermute | solution.py:23
  99.2 32.7 %collective-permute-start.17 = (f32[50,50,1]{1,2,0:T(1,128)}, f32[50,50,1]{1,2,0:T(1,128)}, u32[]{:S(2)}, u32[]{:S(2)}) collective-permute-start(f32[50,50,1]{1,2,0:T(1,128)} %copy.15), channel_id=1, source_target_pairs={{0,1},{1,2},{2,3},{4,5},{5,6},{6,7},{8,9},{9,10},{10,11},{12,13},{... | collective-permute-start | bytes 30008 | tf_op jit(solution)/shard_map/ppermute | solution.py:20
  174.4 7.2 collective-permute-start.20
  175.7 7.3 collective-permute-start.21
  183.2 13.1 %collective-permute-start.22 = (f32[26,26,1]{2,1,0:T(8,128)S(1)}, f32[26,26,1]{2,1,0:T(8,128)S(1)}, u32[]{:S(2)}, u32[]{:S(2)}) collective-permute-start(f32[26,26,1]{2,1,0:T(8,128)S(1)} %get-tuple-element.66), channel_id=1, source_target_pairs={{1,0},{2,1},{3,2},{5,4},{6,5},{7,6},{9,8},{10,9},{11,10},{13,12},{... | collective-permute-start | bytes 8120 | tf_op jit(solution)/shard_map/ppermute | solution.py:23
  184.5 13.0 %collective-permute-start.23 = (f32[26,26,1]{2,1,0:T(8,128)S(1)}, f32[26,26,1]{2,1,0:T(8,128)S(1)}, u32[]{:S(2)}, u32[]{:S(2)}) collective-permute-start(f32[26,26,1]{2,1,0:T(8,128)S(1)} %get-tuple-element.67), channel_id=1, source_target_pairs={{0,1},{1,2},{2,3},{4,5},{5,6},{6,7},{8,9},{9,10},{10,11},{12,13},{... | collective-permute-start | bytes 8120 | tf_op jit(solution)/shard_map/ppermute | solution.py:20
  203.2 7.1 collective-permute-start.26
  204.5 7.1 collective-permute-start.27
  213.3 14.7 %collective-permute-start.28 = (f32[26,26,1]{2,1,0:T(8,128)}, f32[26,26,1]{2,1,0:T(8,128)}, u32[]{:S(2)}, u32[]{:S(2)}) collective-permute-start(f32[26,26,1]{2,1,0:T(8,128)} %get-tuple-element.64), channel_id=1, source_target_pairs={{1,0},{2,1},{3,2},{5,4},{6,5},{7,6},{9,8},{10,9},{11,10},{13,12},{... | collective-permute-start | bytes 8120 | tf_op jit(solution)/shard_map/ppermute | solution.py:23
  214.6 13.9 %collective-permute-start.29 = (f32[26,26,1]{2,1,0:T(8,128)}, f32[26,26,1]{2,1,0:T(8,128)}, u32[]{:S(2)}, u32[]{:S(2)}) collective-permute-start(f32[26,26,1]{2,1,0:T(8,128)} %get-tuple-element.65), channel_id=1, source_target_pairs={{0,1},{1,2},{2,3},{4,5},{5,6},{6,7},{8,9},{9,10},{10,11},{12,13},{... | collective-permute-start | bytes 8120 | tf_op jit(solution)/shard_map/ppermute | solution.py:20
  254.8 7.3 collective-permute-start.34
  256.1 7.5 collective-permute-start.35
  271.9 7.3 collective-permute-start.38
  273.2 7.0 collective-permute-start.39
  281.9 10.7 %collective-permute-start.40 = (f32[14,14,1]{2,1,0:T(8,128)}, f32[14,14,1]{2,1,0:T(8,128)}, u32[]{:S(2)}, u32[]{:S(2)}) collective-permute-start(f32[14,14,1]{2,1,0:T(8,128)} %get-tuple-element.94), channel_id=1, source_target_pairs={{1,0},{2,1},{3,2},{5,4},{6,5},{7,6},{9,8},{10,9},{11,10},{13,12},{... | collective-permute-start | bytes 2360 | tf_op jit(solution)/shard_map/ppermute | solution.py:23
  283.1 9.5 %collective-permute-start.41 = (f32[14,14,1]{2,1,0:T(8,128)}, f32[14,14,1]{2,1,0:T(8,128)}, u32[]{:S(2)}, u32[]{:S(2)}) collective-permute-start(f32[14,14,1]{2,1,0:T(8,128)} %get-tuple-element.95), channel_id=1, source_target_pairs={{0,1},{1,2},{2,3},{4,5},{5,6},{6,7},{8,9},{9,10},{10,11},{12,13},{... | collective-permute-start | bytes 2360 | tf_op jit(solution)/shard_map/ppermute | solution.py:20
  307.1 10.0 %collective-permute-start.44 = (f32[8,1,6]{2,1,0:T(1,128)}, f32[8,1,6]{2,1,0:T(1,128)}, u32[]{:S(2)}, u32[]{:S(2)}) collective-permute-start(f32[8,1,6]{2,1,0:T(1,128)} %get-tuple-element.127), channel_id=1, source_target_pairs={{4,0},{8,4},{12,8},{5,1},{9,5},{13,9},{6,2},{10,6},{14,10},{7,3},{... | collective-permute-start | bytes 584 | tf_op jit(solution)/shard_map/ppermute | solution.py:23
  308.4 8.8 %collective-permute-start.45 = (f32[8,1,6]{2,1,0:T(1,128)}, f32[8,1,6]{2,1,0:T(1,128)}, u32[]{:S(2)}, u32[]{:S(2)}) collective-permute-start(f32[8,1,6]{2,1,0:T(1,128)} %get-tuple-element.126), channel_id=1, source_target_pairs={{0,4},{4,8},{8,12},{1,5},{5,9},{9,13},{2,6},{6,10},{10,14},{3,7},{... | collective-permute-start | bytes 584 | tf_op jit(solution)/shard_map/ppermute | solution.py:20
  318.0 7.7 collective-permute-start.46
  335.1 18.3 %collective-permute-start.50 = (f32[8,1,6]{2,1,0:T(1,128)}, f32[8,1,6]{2,1,0:T(1,128)}, u32[]{:S(2)}, u32[]{:S(2)}) collective-permute-start(f32[8,1,6]{2,1,0:T(1,128)} %get-tuple-element.123), channel_id=1, source_target_pairs={{4,0},{8,4},{12,8},{5,1},{9,5},{13,9},{6,2},{10,6},{14,10},{7,3},{... | collective-permute-start | bytes 584 | tf_op jit(solution)/shard_map/ppermute | solution.py:23
  336.4 17.1 %collective-permute-start.51 = (f32[8,1,6]{2,1,0:T(1,128)}, f32[8,1,6]{2,1,0:T(1,128)}, u32[]{:S(2)}, u32[]{:S(2)}) collective-permute-start(f32[8,1,6]{2,1,0:T(1,128)} %get-tuple-element.122), channel_id=1, source_target_pairs={{0,4},{4,8},{8,12},{1,5},{5,9},{9,13},{2,6},{6,10},{10,14},{3,7},{... | collective-permute-start | bytes 584 | tf_op jit(solution)/shard_map/ppermute | solution.py:20
  354.3 21.1 %collective-permute-start.52 = (f32[8,8,1]{2,1,0:T(8,128)S(1)}, f32[8,8,1]{2,1,0:T(8,128)S(1)}, u32[]{:S(2)}, u32[]{:S(2)}) collective-permute-start(f32[8,8,1]{2,1,0:T(8,128)S(1)} %get-tuple-element.120), channel_id=1, source_target_pairs={{1,0},{2,1},{3,2},{5,4},{6,5},{7,6},{9,8},{10,9},{11,10},{13,12},{... | collective-permute-start | bytes 776 | tf_op jit(solution)/shard_map/ppermute | solution.py:23
  355.6 19.8 %collective-permute-start.53 = (f32[8,8,1]{2,1,0:T(8,128)S(1)}, f32[8,8,1]{2,1,0:T(8,128)S(1)}, u32[]{:S(2)}, u32[]{:S(2)}) collective-permute-start(f32[8,8,1]{2,1,0:T(8,128)S(1)} %get-tuple-element.121), channel_id=1, source_target_pairs={{0,1},{1,2},{2,3},{4,5},{5,6},{6,7},{8,9},{9,10},{10,11},{12,13},{... | collective-permute-start | bytes 776 | tf_op jit(solution)/shard_map/ppermute | solution.py:20
  510.7 7.0 collective-permute-start.70
  512.0 7.2 collective-permute-start.71
  524.6 7.0 collective-permute-start.74
  525.9 7.1 collective-permute-start.75
  533.1 7.1 collective-permute-start.76
  534.4 7.3 collective-permute-start.77
  555.1 7.2 collective-permute-start.80
  556.4 7.3 collective-permute-start.81
  563.9 13.8 %collective-permute-start.82 = (f32[26,26,1]{2,1,0:T(8,128)S(1)}, f32[26,26,1]{2,1,0:T(8,128)S(1)}, u32[]{:S(2)}, u32[]{:S(2)}) collective-permute-start(f32[26,26,1]{2,1,0:T(8,128)S(1)} %get-tuple-element.62), channel_id=1, source_target_pairs={{1,0},{2,1},{3,2},{5,4},{6,5},{7,6},{9,8},{10,9},{11,10},{13,12},{... | collective-permute-start | bytes 8120 | tf_op jit(solution)/shard_map/ppermute | solution.py:23
  565.2 13.7 %collective-permute-start.83 = (f32[26,26,1]{2,1,0:T(8,128)S(1)}, f32[26,26,1]{2,1,0:T(8,128)S(1)}, u32[]{:S(2)}, u32[]{:S(2)}) collective-permute-start(f32[26,26,1]{2,1,0:T(8,128)S(1)} %get-tuple-element.63), channel_id=1, source_target_pairs={{0,1},{1,2},{2,3},{4,5},{5,6},{6,7},{8,9},{9,10},{10,11},{12,13},{... | collective-permute-start | bytes 8120 | tf_op jit(solution)/shard_map/ppermute | solution.py:20
  584.6 7.0 collective-permute-start.86
  585.9 7.1 collective-permute-start.87
  593.3 13.9 %collective-permute-start.88 = (f32[26,26,1]{2,1,0:T(8,128)S(1)}, f32[26,26,1]{2,1,0:T(8,128)S(1)}, u32[]{:S(2)}, u32[]{:S(2)}) collective-permute-start(f32[26,26,1]{2,1,0:T(8,128)S(1)} %get-tuple-element.60), channel_id=1, source_target_pairs={{1,0},{2,1},{3,2},{5,4},{6,5},{7,6},{9,8},{10,9},{11,10},{13,12},{... | collective-permute-start | bytes 8120 | tf_op jit(solution)/shard_map/ppermute | solution.py:23
  594.6 13.7 %collective-permute-start.89 = (f32[26,26,1]{2,1,0:T(8,128)S(1)}, f32[26,26,1]{2,1,0:T(8,128)S(1)}, u32[]{:S(2)}, u32[]{:S(2)}) collective-permute-start(f32[26,26,1]{2,1,0:T(8,128)S(1)} %get-tuple-element.61), channel_id=1, source_target_pairs={{0,1},{1,2},{2,3},{4,5},{5,6},{6,7},{8,9},{9,10},{10,11},{12,13},{... | collective-permute-start | bytes 8120 | tf_op jit(solution)/shard_map/ppermute | solution.py:20
  655.7 9.6 %collective-permute-start.94 = (f32[50,50,1]{1,2,0:T(1,128)}, f32[50,50,1]{1,2,0:T(1,128)}, u32[]{:S(2)}, u32[]{:S(2)}) collective-permute-start(f32[50,50,1]{1,2,0:T(1,128)} %copy.22), channel_id=1, source_target_pairs={{1,0},{2,1},{3,2},{5,4},{6,5},{7,6},{9,8},{10,9},{11,10},{13,12},{... | collective-permute-start | bytes 30008 | tf_op jit(solution)/shard_map/ppermute | solution.py:23
  659.5 8.2 %collective-permute-start.95 = (f32[50,50,1]{1,2,0:T(1,128)}, f32[50,50,1]{1,2,0:T(1,128)}, u32[]{:S(2)}, u32[]{:S(2)}) collective-permute-start(f32[50,50,1]{1,2,0:T(1,128)} %copy.24), channel_id=1, source_target_pairs={{0,1},{1,2},{2,3},{4,5},{5,6},{6,7},{8,9},{9,10},{10,11},{12,13},{... | collective-permute-start | bytes 30008 | tf_op jit(solution)/shard_map/ppermute | solution.py:20
  682.9 7.0 collective-permute-start.99
  694.4 7.8 collective-permute-start.100
  720.2 7.3 collective-permute-start.104
  721.5 7.3 collective-permute-start.105
  734.1 9.0 %collective-permute-start.106 = (f32[50,50,1]{1,2,0:T(1,128)}, f32[50,50,1]{1,2,0:T(1,128)}, u32[]{:S(2)}, u32[]{:S(2)}) collective-permute-start(f32[50,50,1]{1,2,0:T(1,128)} %copy.30), channel_id=1, source_target_pairs={{1,0},{2,1},{3,2},{5,4},{6,5},{7,6},{9,8},{10,9},{11,10},{13,12},{... | collective-permute-start | bytes 30008 | tf_op jit(solution)/shard_map/ppermute | solution.py:23
  737.8 7.7 collective-permute-start.107
  (112 other events, 706.9 us)
where the time goes:
time: 820 us; the launch traced here: 805 us
  starting transfers between devices  315 us (38%)
  local copies, waits for them, and re-layouts  164 us (20%)
  other arithmetic  142 us (17%)
  blocking collectives  95.1 us (12%)
  waiting for transfers between devices  71.6 us (9%)
  between operations  18.1 us (2%)
    ppermute x54, starting transfers between devices, extended(): lax.ppermute(lax.slice_in_dim(block, block.shape[dim] - width, None, axis...  246 us
    ppermute x54, starting transfers between devices, extended(): lax.ppermute(lax.slice_in_dim(block, 0, width, axis=dim), axis, backward)  69.6 us
    ppermute x54, waiting for transfers between devices, extended(): lax.ppermute(lax.slice_in_dim(block, block.shape[dim] - width, None, axis...  46.4 us
    psum x1, blocking collectives, body(): upper = lax.psum(jnp.sum(start_residual * precond), ('gx', 'gy', 'gz'))  44.6 us
    reshape x5, local copies, waits for them, and re-layouts, coarsen(): blocks = values.reshape(size_x // 2, 2, size_y // 2, 2, size_z // 2, 2)  36.5 us
    reduce_sum x8, other arithmetic, coarsen(): return jnp.mean(blocks, axis=(1, 3, 5))  34.2 us
    add x12, other arithmetic, vcycle_level(): estimate + damping * (source - operator(estimate, shifted, factor)) / dia...  29.9 us
    slice x25, local copies, waits for them, and re-layouts, extended(): lax.slice_in_dim(block, 0, width, axis=dim)  28.5 us
  transfers between devices with their start and end apart: 108, of which 49 were waited for; matrix products, arithmetic and copies ran while one was open for 8% of the time, Pallas kernels for 0%

commit v1 on v0

v1 whole, which is shorter than its diff:
```python
import jax
import jax.numpy as jnp
from jax import lax
from jax.experimental import pallas as pl
from jax.experimental.pallas import tpu as pltpu
from jax.sharding import PartitionSpec as P

LEVELS = 5
BOTTOM_ITERS = 6
LOCAL = 2
AXES = ("gx", "gy", "gz")
MESH = pl.DeviceIdType.MESH
F32 = jnp.float32

damping = 6.0 / 7.0


def up_to(n, m):
    return -(-n // m) * m


def lanes_of(shape):
    return up_to(max(shape[2] + 1, shape[0]), 128)


def halved(shape, times):
    return tuple(s >> times for s in shape)


def loop(n, f, carry=0, unroll=4):
    while n % unroll:
        unroll -= 1

    def step(i, c):
        for k in range(unroll):
            c = f(i * unroll + k, c)
        return c

    return lax.fori_loop(0, n // unroll, step, carry)


def lane_of(rows, lanes):
    return lax.broadcasted_iota(jnp.int32, (rows, lanes), 1)


def pick(lanes_in, lanes_out, f, value):
    r = lax.broadcasted_iota(jnp.int32, (lanes_in, lanes_out), 0)
    c = lax.broadcasted_iota(jnp.int32, (lanes_in, lanes_out), 1)
    return jnp.where(f(r, c), value, 0.0).astype(F32)


def dot(a, b):
    return lax.dot(a, b, precision=lax.Precision.HIGHEST, preferred_element_type=F32)


def total(v):
    v = jnp.sum(v, axis=0, keepdims=True)
    return jnp.sum(v, axis=1, keepdims=True)


def fold(v):
    out = v[0:8]
    for k in range(1, v.shape[0] // 8):
        out = out + v[8 * k : 8 * k + 8]
    return out


def make_kernel(sizes, block):
    nx, ny, nz = sizes
    whole = (block[0] * nx, block[1] * ny, block[2] * nz)
    shapes = [halved(block, k) if k < LOCAL else halved(whole, k) for k in range(LEVELS)]
    lanes = [lanes_of(s) for s in shapes]
    counts = [6, 4]
    part = halved(block, LOCAL)
    wide = shapes[LOCAL][2]
    packs = 2 if wide <= 64 and part[0] % 2 == 0 else 1
    slabs = part[0] // packs
    rows = up_to(part[1], 8)
    glanes = lanes[LOCAL]
    half = glanes // packs

    scratch = {}
    for k in range(LEVELS):
        X, Y, Z = shapes[k]
        L = lanes[k]
        Yp = up_to(Y, 8)
        n = counts[k] if k < LOCAL else 2
        scratch[f"e{k}"] = pltpu.VMEM((n, X + 2, Yp + 16, L), F32)
        scratch[f"f{k}"] = pltpu.VMEM((X, Yp, L), F32)
        scratch[f"s{k}"] = pltpu.VMEM((X, Yp, L), F32)
        scratch[f"w{k}"] = pltpu.VMEM((X, Yp, L), F32)
        if k < LEVELS - 1:
            scratch[f"t{k}"] = pltpu.VMEM((L // 128, X // 2, 2 * up_to(Y // 2, 8), 128), F32)
        if k < LOCAL:
            for name, n_rows in (("zs", Y), ("zr", Y), ("ys", X), ("yr", X)):
                scratch[f"{name}{k}"] = pltpu.VMEM((n, 2, n_rows, L), F32)
            scratch[f"send{k}"] = pltpu.SemaphoreType.DMA((n, 6))
            scratch[f"recv{k}"] = pltpu.SemaphoreType.DMA((n, 6))
    scratch["ap"] = pltpu.VMEM((block[0], block[1], lanes[0]), F32)
    for g in range(2):
        scratch[f"gz{g}"] = pltpu.VMEM((nz, slabs, rows, glanes), F32)
        scratch[f"gm{g}"] = pltpu.VMEM((slabs, rows, glanes), F32)
        scratch[f"gy{g}"] = pltpu.VMEM((slabs, ny * rows, glanes), F32)
        scratch[f"gx{g}"] = pltpu.VMEM((nx, slabs, ny * rows, glanes), F32)
    for i, n in enumerate(sizes):
        scratch[f"q{i}"] = pltpu.VMEM((n, 16, lanes[0]), F32)
        scratch[f"qs{i}"] = pltpu.VMEM((16, lanes[0]), F32)
    scratch["gsend"] = pltpu.SemaphoreType.DMA((3, 3, max(sizes)))
    scratch["grecv"] = pltpu.SemaphoreType.DMA((3, 3, max(sizes)))

    names = list(scratch)

    def kernel(rs_ref, sg_ref, re_ref, sol_ref, res_ref, *refs):
        R = dict(zip(names, refs))
        pos = [lax.axis_index(a) for a in AXES]

        def zero(ref):
            ref[...] = jnp.zeros(ref.shape, F32)

        for k in range(LEVELS):
            X, Y, Z = shapes[k]
            for b in range(R[f"e{k}"].shape[0]):
                zero(R[f"e{k}"].at[b, 0])
                zero(R[f"e{k}"].at[b, X + 1])
                if k >= LOCAL:
                    Yp = up_to(Y, 8)
                    for x in range(1, X + 1):
                        R[f"e{k}"][b, x, 0:8, :] = jnp.zeros((8, lanes[k]), F32)
                        R[f"e{k}"][b, x, Yp + 8 :, :] = jnp.zeros((8, lanes[k]), F32)
                else:
                    zero(R[f"zr{k}"].at[b, 0])
                    zero(R[f"zr{k}"].at[b, 1])
                    zero(R[f"yr{k}"].at[b, 0])
                    zero(R[f"yr{k}"].at[b, 1])
            if k < LEVELS - 1 and Y // 2 % 8:
                for m in range(lanes[k] // 128):
                    for x in range(X // 2):
                        R[f"t{k}"][m, x, Y:, :] = jnp.zeros((R[f"t{k}"].shape[2] - Y, 128), F32)

        barrier = pltpu.get_barrier_semaphore()
        for axis, n, me in zip(AXES, sizes, pos):
            for d in range(1, n):
                pl.semaphore_signal(barrier, inc=1, device_id={axis: lax.rem(me + d, n)}, device_id_type=MESH)
        pl.semaphore_wait(barrier, sum(n - 1 for n in sizes))

        pending = []

        def copies(k, b):
            X, Y, Z = shapes[k]
            e = R[f"e{k}"]
            zs, zr, ys, yr = (R[f"{m}{k}"] for m in ("zs", "zr", "ys", "yr"))
            out = []
            pairs = (
                (e.at[b, 1, pl.ds(8, Y), :], e.at[b, X + 1, pl.ds(8, Y), :]),
                (e.at[b, X, pl.ds(8, Y), :], e.at[b, 0, pl.ds(8, Y), :]),
                (ys.at[b, 0], yr.at[b, 1]),
                (ys.at[b, 1], yr.at[b, 0]),
                (zs.at[b, 0], zr.at[b, 1]),
                (zs.at[b, 1], zr.at[b, 0]),
            )
            for i, (src, dst) in enumerate(pairs):
                axis, me, n = AXES[i // 2], pos[i // 2], sizes[i // 2]
                target = me - 1 if i % 2 == 0 else me + 1
                low, high = me > 0, me < n - 1
                copy = pltpu.make_async_remote_copy(
                    src_ref=src,
                    dst_ref=dst,
                    send_sem=R[f"send{k}"].at[b, i],
                    recv_sem=R[f"recv{k}"].at[b, i],
                    device_id={axis: target},
                    device_id_type=MESH,
                )
                out.append((copy, low if i % 2 == 0 else high, high if i % 2 == 0 else low))
            return out

        def send(k, b):
            for copy, sends, _ in copies(k, b):
                pl.when(sends)(copy.start)
            pending.append((k, b))

        def receive(k, b):
            X, Y, Z = shapes[k]
            for copy, _, receives in copies(k, b):
                pl.when(receives)(copy.wait_recv)
            for x in range(X):
                R[f"e{k}"][b, x + 1, 7:8, :] = R[f"yr{k}"][b, 0, x : x + 1, :]
                R[f"e{k}"][b, x + 1, 8 + Y : 9 + Y, :] = R[f"yr{k}"][b, 1, x : x + 1, :]

        def applied(k, b, x, split):
            X, Y, Z = shapes[k]
            L = lanes[k]
            Yp = up_to(Y, 8)
            e = R[f"e{k}"]
            i = x + 1
            c = e[b, i, 8 : 8 + Yp, :]
            beside = e[b, i + 1, 8 : 8 + Yp, :] + e[b, i - 1, 8 : 8 + Yp, :]
            beside = beside + (e[b, i, 9 : 9 + Yp, :] + e[b, i, 7 : 7 + Yp, :])
            beside = beside + (pltpu.roll(c, 1, 1) + pltpu.roll(c, L - 1, 1))
            if split:
                lane = lane_of(Yp, L)
                low = pltpu.roll(R[f"zr{k}"][b, 0], lax.rem(L - x, L), 1)
                high = pltpu.roll(R[f"zr{k}"][b, 1], lax.rem(L + Z - 1 - x, L), 1)
                beside = beside + jnp.where(lane == 0, low, jnp.where(lane == Z - 1, high, 0.0))
            return c, 0.25**k * (6.0 * c - beside) + R[f"s{k}"][x] * c

        def produce(k, b, f):
            X, Y, Z = shapes[k]
            L = lanes[k]
            lane = lane_of(Y, L)

            def one(x, faces):
                low, high = faces
                v = f(x)
                R[f"e{k}"][b, x + 1, 8 : 8 + Y, :] = v
                R[f"ys{k}"][b, 0, pl.ds(x, 1), :] = v[0:1]
                R[f"ys{k}"][b, 1, pl.ds(x, 1), :] = v[Y - 1 : Y]
                low = jnp.where(lane == x, pltpu.roll(v, x, 1), low)
                high = jnp.where(lane == x, pltpu.roll(v, lax.rem(x + L - Z + 1, L), 1), high)
                return low, high

            low, high = loop(X, one, (jnp.zeros((Y, L), F32), jnp.zeros((Y, L), F32)))
            R[f"zs{k}"][b, 0] = low
            R[f"zs{k}"][b, 1] = high
            send(k, b)

        def relaxed(k, b, x, split):
            c, a = applied(k, b, x, split)
            return c + R[f"w{k}"][x] * (R[f"f{k}"][x] - a)

        def keep(k, j, n, v):
            for m in range(lanes[k] // 128):
                R[f"t{k}"][m, j, 0:n, :] = v[:, 128 * m : 128 * m + 128]

        def kept(k, j, n):
            v = [R[f"t{k}"][m, j, 0:n, :] for m in range(lanes[k] // 128)]
            return v[0] if len(v) == 1 else jnp.concatenate(v, axis=1)

        def double_rows(k, v):
            n = v.shape[1]
            for m in range(lanes[k] // 128):
                for d in range(2):
                    R[f"t{k}"][m, :, pl.ds(d, n, stride=2), :] = v[:, :, 128 * m : 128 * m + 128]

        def pairs_of(k, f):
            X, Y, Z = shapes[k]

            def one(j, c):
                keep(k, j, up_to(Y, 8), f(2 * j) + f(2 * j + 1))
                return c

            loop(X // 2, one, 0, 2)

        def halve_rows(k):
            t = R[f"t{k}"]
            n = t.shape[2] // 2
            v = [
                t[m, :, pl.ds(0, n, stride=2), :] + t[m, :, pl.ds(1, n, stride=2), :]
                for m in range(lanes[k] // 128)
            ]
            v = [u.reshape(u.shape[0] * n, 128) for u in v]
            return v[0] if len(v) == 1 else jnp.concatenate(v, axis=1)

        def coarsened(k):
            X, Y, Z = shapes[k]
            n = R[f"t{k}"].shape[2] // 2
            C = pick(lanes[k], lanes[k + 1], lambda r, c: (r // 2 == c) & (r < Z), 0.125)
            return dot(halve_rows(k), C).reshape(X // 2, n, lanes[k + 1])

        def weights(k):
            X, Y, Z = shapes[k]
            Yp = up_to(Y, 8)
            lane = lane_of(Yp, lanes[k])

            def one(x, c):
                s = jnp.where(lane < Z, R[f"s{k}"][x], 0.0)
                R[f"w{k}"][x] = jnp.where(lane < Z, damping / (6.0 * 0.25**k + s), 0.0)
                return c

            loop(X, one)

        def spread(g, stage):
            axis_at = 2 - stage
            axis, n, me = AXES[axis_at], sizes[axis_at], pos[axis_at]
            if stage == 0:
                src, dst = R[f"gz{g}"].at[me], R[f"gz{g}"].at[me]
            elif stage == 1:
                here = pl.ds(pl.multiple_of(me * rows, 8), rows)
                src, dst = R[f"gm{g}"], R[f"gy{g}"].at[:, here, :]
            else:
                src, dst = R[f"gy{g}"], R[f"gx{g}"].at[me]
            return [
                pltpu.make_async_remote_copy(
                    src_ref=src,
                    dst_ref=dst,
                    send_sem=R["gsend"].at[g, stage, d],
                    recv_sem=R["grecv"].at[g, stage, d],
                    device_id={axis: lax.rem(me + d, n)},
                    device_id_type=MESH,
                )
                for d in range(1, n)
            ]

        def gather_first(g):
            k = LOCAL - 1
            Z = shapes[k][2]
            v = halve_rows(k)
            v = v.reshape(packs, slabs * rows, v.shape[1])
            block_sum = None
            for h in range(packs):
                at = pos[2] * part[2] + h * half
                C = pick(lanes[k], glanes, lambda r, c: (r // 2 + at == c) & (r < Z), 0.125)
                piece = dot(v[h], C)
                block_sum = piece if block_sum is None else block_sum + piece
            R[f"gz{g}"][pos[2]] = block_sum.reshape(slabs, rows, glanes)
            for copy in spread(g, 0):
                copy.start()

        def gather_second(g):
            for copy in spread(g, 0):
                copy.wait_recv()
            v = R[f"gz{g}"][0]
            for i in range(1, nz):
                v = v + R[f"gz{g}"][i]
            R[f"gm{g}"][...] = v
            for copy in spread(g, 1):
                copy.start()
            R[f"gy{g}"][:, pl.ds(pl.multiple_of(pos[1] * rows, 8), rows), :] = v

        def gather_third(g):
            for copy in spread(g, 1):
                copy.wait_recv()
            for copy in spread(g, 2):
                copy.start()

        def gather_last(g, name):
            k = LOCAL
            lane = lane_of(part[1], glanes)
            R[f"gx{g}"][pos[0]] = R[f"gy{g}"][...]
            for copy in spread(g, 2):
                copy.wait_recv()
            for i in range(nx):
                for h in range(packs):
                    for j in range(slabs):
                        x = (i * packs + h) * slabs + j
                        for m in range(ny):
                            v = R[f"gx{g}"][i, j, m * rows : m * rows + part[1], :]
                            if h:
                                v = pltpu.roll(v, glanes - h * half, 1)
                            if packs > 1:
                                v = jnp.where(lane < wide, v, 0.0)
                            R[f"{name}{k}"][x, m * part[1] : (m + 1) * part[1], :] = v

        def gather_sends(g):
            for stage in range(3):
                for copy in spread(g, stage):
                    copy.wait_send()

        X, Y, Z = block
        L = lanes[0]

        def fill_guess(x):
            v = sg_ref[x]
            return jnp.concatenate([v, jnp.zeros((Y, L - Z), F32)], axis=1)

        produce(0, 0, fill_guess)

        def fill(x, c):
            v = jnp.concatenate([re_ref[x], jnp.zeros((Y, L - Z), F32)], axis=1)
            R["s0"][x] = v
            return c

        loop(X, fill)
        weights(0)
        for k in range(LOCAL):
            pairs_of(k, lambda x: R[f"s{k}"][x])
            if k < LOCAL - 1:
                R[f"s{k + 1}"][...] = coarsened(k)
                weights(k + 1)
            else:
                gather_first(0)

        receive(0, 0)

        def residual_of(x):
            c, a = applied(0, 0, x, True)
            f = jnp.concatenate([rs_ref[x], jnp.zeros((Y, L - Z), F32)], axis=1) - a
            R["f0"][x] = f
            return R["w0"][x] * f

        produce(0, 1, residual_of)
        gather_second(0)
        receive(0, 1)
        produce(0, 2, lambda x: relaxed(0, 1, x, True))
        gather_third(0)

        def left(k, b, x, split):
            c, a = applied(k, b, x, split)
            return R[f"f{k}"][x] - a

        receive(0, 2)
        pairs_of(0, lambda x: left(0, 2, x, True))
        R["f1"][...] = coarsened(0)
        produce(1, 0, lambda x: R["w1"][x] * R["f1"][x])
        gather_last(0, "s")
        for k in range(LOCAL, LEVELS):
            weights(k)
            if k < LEVELS - 1:
                pairs_of(k, lambda x: R[f"s{k}"][x])
                R[f"s{k + 1}"][...] = coarsened(k)
        receive(1, 0)
        produce(1, 1, lambda x: relaxed(1, 0, x, True))
        receive(1, 1)
        pairs_of(1, lambda x: left(1, 1, x, True))
        gather_first(1)
        gather_second(1)
        gather_third(1)
        gather_last(1, "f")

        def solve(k):
            X, Y, Z = shapes[k]
            Yp, L = up_to(Y, 8), lanes[k]
            e, f, w = R[f"e{k}"], R[f"f{k}"], R[f"w{k}"]

            def put(b, g):
                def one(x, c):
                    e[b, x + 1, 8 : 8 + Yp, :] = g(x)
                    return c

                loop(X, one)

            if k == LEVELS - 1:
                inside = (lane_of(Yp, L) < Z) & (lax.broadcasted_iota(jnp.int32, (Yp, L), 0) < Y)
                r = [jnp.where(inside, f[x], 0.0) for x in range(X)]
                p = list(r)
                answer = [jnp.zeros((Yp, L), F32) for _ in range(X)]

                def inner(u, v):
                    s = u[0] * v[0]
                    for x in range(1, X):
                        s = s + u[x] * v[x]
                    return total(s)

                rr = inner(r, r)
                for _ in range(BOTTOM_ITERS):
                    for x in range(X):
                        e[0, x + 1, 8 : 8 + Yp, :] = p[x]
                    q = [jnp.where(inside, applied(k, 0, x, False)[1], 0.0) for x in range(X)]
                    a = rr / inner(p, q)
                    answer = [u + a * v for u, v in zip(answer, p)]
                    r = [u - a * v for u, v in zip(r, q)]
                    new = inner(r, r)
                    ratio = new / rr
                    p = [u + ratio * v for u, v in zip(r, p)]
                    rr = new
                for x in range(X):
                    e[1, x + 1, 8 : 8 + Yp, :] = answer[x]
                return
            put(0, lambda x: w[x] * f[x])
            put(1, lambda x: relaxed(k, 0, x, False))
            pairs_of(k, lambda x: left(k, 1, x, False))
            R[f"f{k + 1}"][...] = coarsened(k)
            solve(k + 1)
            prolong(k)
            put(0, lambda x: e[1, x + 1, 8 : 8 + Yp, :] + kept(k, x // 2, Yp))
            put(1, lambda x: relaxed(k, 0, x, False))
            put(0, lambda x: relaxed(k, 1, x, False))

        def prolong(k):
            X, Y, Z = shapes[k]
            Yc = up_to(Y // 2, 8)
            b = 1 if k + 1 == LEVELS - 1 else 0
            C = pick(lanes[k + 1], lanes[k], lambda r, c: (c // 2 == r) & (c < Z), 1.0)
            v = R[f"e{k + 1}"][b, 1 : X // 2 + 1, 8 : 8 + Yc, :]
            v = dot(v.reshape(X // 2 * Yc, lanes[k + 1]), C).reshape(X // 2, Yc, lanes[k])
            double_rows(k, v)

        solve(LOCAL)

        k = LOCAL - 1
        Xk, Yk, Zk = shapes[k]
        C = pick(glanes, lanes[k], lambda r, c: (c // 2 + pos[2] * part[2] == r) & (c < Zk), 1.0)
        B = pick(Yk, shapes[LOCAL][1], lambda r, c: r // 2 + pos[1] * part[1] == c, 1.0)
        for j in range(Xk // 2):
            v = R[f"e{LOCAL}"][0, pos[0] * part[0] + j + 1, 8 : 8 + shapes[LOCAL][1], :]
            keep(k, j, Yk, dot(dot(B, v), C))
        produce(1, 2, lambda x: R["e1"][1, x + 1, 8 : 8 + Yk, :] + kept(1, x // 2, Yk))
        receive(1, 2)
        produce(1, 3, lambda x: relaxed(1, 2, x, True))
        receive(1, 3)

        def last_one(x, c):
            v = relaxed(1, 3, x, True)
            R["w1"][x] = v
            return c

        loop(Xk, last_one)
        C = pick(lanes[1], lanes[0], lambda r, c: (c // 2 == r) & (c < Z), 1.0)
        v = dot(R["w1"][...].reshape(Xk * Yk, lanes[1]), C).reshape(Xk, Yk, lanes[0])
        double_rows(0, v)
        produce(0, 3, lambda x: R["e0"][2, x + 1, 8 : 8 + Y, :] + kept(0, x // 2, Y))
        receive(0, 3)
        produce(0, 4, lambda x: relaxed(0, 3, x, True))
        receive(0, 4)
        produce(0, 5, lambda x: relaxed(0, 4, x, True))
        receive(0, 5)

        def image(x, sums):
            upper, lower = sums
            c, a = applied(0, 5, x, True)
            R["ap"][x] = a
            return upper + fold(R["f0"][x] * c), lower + fold(a * c)

        upper, lower = loop(X, image, (jnp.zeros((8, L), F32), jnp.zeros((8, L), F32)))
        for i in range(3):
            n, me = sizes[i], pos[i]
            R[f"qs{i}"][0:8] = upper
            R[f"qs{i}"][8:16] = lower
            sums = [
                pltpu.make_async_remote_copy(
                    src_ref=R[f"qs{i}"],
                    dst_ref=R[f"q{i}"].at[me],
                    send_sem=R["gsend"].at[2, i, d],
                    recv_sem=R["grecv"].at[2, i, d],
                    device_id={AXES[i]: lax.rem(me + d, n)},
                    device_id_type=MESH,
                )
                for d in range(1, n)
            ]
            for copy in sums:
                copy.start()
            R[f"q{i}"][me] = R[f"qs{i}"][...]
            for copy in sums:
                copy.wait_recv()
            v = R[f"q{i}"][0]
            for d in range(1, n):
                v = v + R[f"q{i}"][d]
            upper, lower = v[0:8], v[8:16]
            for copy in sums:
                copy.wait_send()
        step_length = total(upper) / total(lower)

        def finish(x, c):
            p = R["e0"][5, x + 1, 8 : 8 + Y, :]
            sol_ref[x] = sg_ref[x] + (step_length * p)[:, 0:Z]
            res_ref[x] = (R["f0"][x] - step_length * R["ap"][x])[:, 0:Z]
            return c

        loop(X, finish)
        for k, b in pending:
            for copy, sends, _ in copies(k, b):
                pl.when(sends)(copy.wait_send)
        gather_sends(0)
        gather_sends(1)

    return kernel, list(scratch.values())


def solution(mesh):
    sizes = tuple(mesh.shape[a] for a in AXES)

    def body(right_side, start_guess, reaction):
        kernel, scratch = make_kernel(sizes, right_side.shape)
        out = jax.ShapeDtypeStruct(right_side.shape, F32)
        return tuple(
            pl.pallas_call(
                kernel,
                out_shape=(out, out),
                in_specs=[pl.BlockSpec(memory_space=pltpu.VMEM)] * 3,
                out_specs=(pl.BlockSpec(memory_space=pltpu.VMEM),) * 2,
                scratch_shapes=scratch,
                compiler_params=pltpu.CompilerParams(
                    collective_id=0, has_side_effects=True, vmem_limit_bytes=60 * 2**20
                ),
                name="cg_step",
            )(right_side, start_guess, reaction)
        )

    placed = P(*AXES)
    return jax.shard_map(
        body, mesh=mesh, in_specs=(placed,) * 3, out_specs=(placed,) * 2, check_vma=False
    )
```

time: 820 us -> 104 us (0.13); the launches traced: 805 us -> 104 us
  starting transfers between devices: 315 us -> 0 us
  local copies, waits for them, and re-layouts: 164 us -> 3.47 us
  other arithmetic: 142 us -> 0 us
  Pallas kernels: 0 us -> 100 us
  blocking collectives: 95.1 us -> 0 us
  waiting for transfers between devices: 71.6 us -> 0 us
  between operations: 18.1 us -> 0.65 us
    ppermute x108 -> x0, starting transfers between devices: 315 us -> none  [the longest x54 246 us: extended(): lax.ppermute(lax.slice_in_dim(block, block.shape[dim] - width, None, axis...]
    pallas_call x0 -> x1, Pallas kernels: none -> 100 us  [body(): pl.pallas_call(kernel, out_shape=(out, out), in_specs=[pl.BlockSpec(memor...]
    ppermute x108 -> x0, waiting for transfers between devices: 71.6 us -> none  [the longest x54 46.4 us: extended(): lax.ppermute(lax.slice_in_dim(block, block.shape[dim] - width, None, axis...]
    reduce_sum x20 -> x0, other arithmetic: 62.8 us -> none  [the longest x8 34.2 us: coarsen(): return jnp.mean(blocks, axis=(1, 3, 5))]
    reshape x9 -> x0, local copies, waits for them, and re-layouts: 61.5 us -> none  [the longest x5 36.5 us: coarsen(): blocks = values.reshape(size_x // 2, 2, size_y // 2, 2, size_z // 2, 2)]
    all_gather x6 -> x0, blocking collectives: 50.5 us -> none  [the longest x1 14.9 us: bottom(): lax.all_gather(gathered[1], 'gz', axis=2, tiled=True)]
    psum x1 -> x0, blocking collectives: 44.6 us -> none  [body(): upper = lax.psum(jnp.sum(start_residual * precond), ('gx', 'gy', 'gz'))]
    slice x49 -> x0, local copies, waits for them, and re-layouts: 41.6 us -> none  [the longest x25 28.5 us: extended(): lax.slice_in_dim(block, 0, width, axis=dim)]
  transfers between devices with their start and end apart: 108 -> 0, of which waited for: 49 -> 0; matrix products, arithmetic and copies ran while one was open for 8% -> 0% of each run, Pallas kernels for 0% -> 0%
where the time goes in v1:
time: 104 us
  Pallas kernels  100 us (96%)
  local copies, waits for them, and re-layouts  3.47 us (3%)
    pallas_call x1, Pallas kernels, body(): pl.pallas_call(kernel, out_shape=(out, out), in_specs=[pl.BlockSpec(memor...  100 us
    unnamed x4, local copies, waits for them, and re-layouts  3.47 us

profile of v1, /device:TPU:0, one launch (start us, length us, event | category | flops | bytes accessed | tf_op | source)
XLA Modules:
  0.0 104.1 jit_solution(13831616499924524828)
XLA Ops:
  0.6 100.0 %cg_step.1 = (f32[48,48,48]{2,1,0:T(8,128)}, f32[48,48,48]{2,1,0:T(8,128)}) custom-call(f32[48,48,48]{2,1,0:T(8,128)} %rs_ref.1, f32[48,48,48]{2,1,0:T(8,128)} %sg_ref.1, f32[48,48,48]{2,1,0:T(8,128)} %re_ref.1), custom_call_target="tpu_custom_call" | custom-call | tf_op jit(solution)/shard_map/cg_step/pallas_call | solution.py:565
  100.7 0.0 copy-start
  100.7 2.5 %copy.7 = f32[48,48,48]{2,1,0:T(8,128)} copy(f32[48,48,48]{2,1,0:T(8,128)} %get-tuple-element.4) | data formatting | bytes 884736
  103.1 0.0 copy-done
  103.1 1.0 copy.8
Async XLA Ops:
  100.7 2.5 %copy-start = (f32[48,48,48]{2,1,0:T(8,128)S(1)}, f32[48,48,48]{2,1,0:T(8,128)}, u32[]{:S(2)}) copy-start(f32[48,48,48]{2,1,0:T(8,128)} %get-tuple-element.5) | copy-start | bytes 1327108
